TPU v7x, 256 devices: a whole 4x4x8 slice. The times are simulated.
256 devices in a mesh: gx: 8 (over z), gy: 32 (over x, y, core).
Axes of the slice: x: 4, y: 4, z: 8, core: 2. Of those that a mesh axis runs over, the one named last changes fastest.
Arguments:
- permeability: float32 [3, 256, 65536], P(None, 'gx', 'gy'), may hold values from 0.03 to 1000, as said below
Outputs:
- fine_pressure: float32 [256, 65536], P('gx', 'gy')
- twin_pressure: float32 [128, 16384], P('gx', 'gy')
Inputs may be any that keep to these rules, and one draw needn't show every extreme that they name: `permeability`: positive conductivities; entry 0, 1, 2 of the first dimension is the conductivity along the grid's first, second, third dimension.
All inputs are finite; a program needn't handle non-finite values.
Results may differ from a plain program's by a relative error of at most 0.0003.
Values sent between devices are 32-bit elements; how exact they have to be, the bound alone decides.
A program may use at most 192 MiB of HBM per device.

v0:
```python
import jax
import jax.numpy as jnp
from jax import lax
from jax.sharding import PartitionSpec as P

EL = 32
ELZ = 16
MX = 4
MZ = 2
EZ = 2
PATCH_ITERS = 3
COARSE_ITERS = 2


def shifted(shard, axis, by):
    count = lax.axis_size(axis)
    return lax.ppermute(shard, axis, [(i, (i + by) % count) for i in range(count)])


def padded_2(cells, sides, width):
    for axis, dim in sides:
        count = lax.axis_size(axis)
        head = lax.slice_in_dim(cells, 0, width, axis=dim)
        tail = lax.slice_in_dim(cells, cells.shape[dim] - width, cells.shape[dim], axis=dim)
        cells = jnp.concatenate(
            [
                lax.ppermute(tail, axis, [(i, (i + 1) % count) for i in range(count)]),
                cells,
                lax.ppermute(head, axis, [((i + 1) % count, i) for i in range(count)]),
            ],
            axis=dim,
        )
    return cells


def harmonic(first, second, spacing):
    return spacing * 2.0 * first * second / (first + second)


def face_weights(conduct, width, spacing):
    weight_rows = harmonic(conduct[0][..., :-width], conduct[0][..., width:], spacing)
    weight_cols = harmonic(conduct[1][..., :-1], conduct[1][..., 1:], spacing)
    column = jnp.arange(weight_cols.shape[-1], dtype=jnp.int32) % width
    weight_cols = jnp.where(column == width - 1, jnp.zeros_like(weight_cols), weight_cols)
    weight_depth = harmonic(conduct[2][:, :-1], conduct[2][:, 1:], spacing)
    return (weight_rows, weight_cols, weight_depth)


def apply_operator(field, weights, width):
    weight_rows, weight_cols, weight_depth = weights
    flux = weight_rows * (field[..., :-width] - field[..., width:])
    result = jnp.pad(flux, ((0, 0), (0, 0), (0, 0), (0, width))) - jnp.pad(
        flux, ((0, 0), (0, 0), (0, 0), (width, 0))
    )
    flux = weight_cols * (field[..., :-1] - field[..., 1:])
    result = (
        result
        + jnp.pad(flux, ((0, 0), (0, 0), (0, 0), (0, 1)))
        - jnp.pad(flux, ((0, 0), (0, 0), (0, 0), (1, 0)))
    )
    flux = weight_depth * (field[:, :, :-1] - field[:, :, 1:])
    result = (
        result
        + jnp.pad(flux, ((0, 0), (0, 0), (0, 1), (0, 0)))
        - jnp.pad(flux, ((0, 0), (0, 0), (1, 0), (0, 0)))
    )
    return result


def interior_mask(depth, rows, width):
    level = jnp.arange(depth, dtype=jnp.int32)[:, None]
    cell = jnp.arange(rows * width, dtype=jnp.int32)[None, :]
    row_index = cell // width
    line_index = cell % width
    inside = (
        (level > 0)
        & (level < depth - 1)
        & (row_index > 0)
        & (row_index < rows - 1)
        & (line_index > 0)
        & (line_index < width - 1)
    )
    return inside.astype(jnp.float32)


def shape_functions(depth, rows, width, edge, edge_depth, margin, margin_depth):
    cell = jnp.arange(rows * width, dtype=jnp.int32)
    place_rows = ((cell // width).astype(jnp.float32) - margin + 0.5) / edge
    place_cols = ((cell % width).astype(jnp.float32) - margin + 0.5) / edge
    place_depth = (
        jnp.arange(depth, dtype=jnp.int32).astype(jnp.float32) - margin_depth + 0.5
    ) / edge_depth
    factors = []
    for basis in range(8):
        along_rows = place_rows if basis // 4 else 1.0 - place_rows
        along_cols = place_cols if basis // 2 % 2 else 1.0 - place_cols
        along_depth = place_depth if basis % 2 else 1.0 - place_depth
        factors.append(along_depth[:, None] * (along_rows * along_cols)[None, :])
    return jnp.stack(factors)[:, None]


def patch_fields(block, edge_depth, margin_depth):
    depth = edge_depth + 2 * margin_depth
    count = (block.shape[3] - 2 * margin_depth) // edge_depth
    pieces = [
        block[:, :, :, index * edge_depth : index * edge_depth + depth] for index in range(count)
    ]
    stacked = jnp.stack(pieces, axis=1)
    return jnp.transpose(stacked, (0, 1, 4, 2, 3)).reshape(
        3, count, depth, block.shape[1] * block.shape[2]
    )


def solve_column(block, edge, edge_depth, margin, margin_depth, spacing):
    rows = block.shape[1]
    width = block.shape[2]
    depth = edge_depth + 2 * margin_depth
    conduct = patch_fields(block, edge_depth, margin_depth)
    count = conduct.shape[1]
    weights = face_weights(conduct, width, spacing)
    inside = interior_mask(depth, rows, width)
    start = shape_functions(depth, rows, width, edge, edge_depth, margin, margin_depth)
    residual = -inside * apply_operator(start, weights, width)
    direction = residual
    norm_now = jnp.sum(residual * residual, axis=(2, 3), keepdims=True)
    update = jnp.zeros_like(residual)
    for step in range(PATCH_ITERS):
        image = inside * apply_operator(direction, weights, width)
        alpha = norm_now / jnp.sum(direction * image, axis=(2, 3), keepdims=True)
        update = update + alpha * direction
        residual = residual - alpha * image
        norm_next = jnp.sum(residual * residual, axis=(2, 3), keepdims=True)
        direction = residual + norm_next / norm_now * direction
        norm_now = norm_next
    solution = start + update
    local = solution.reshape(8, count, depth, rows, width)[
        :,
        :,
        margin_depth : margin_depth + edge_depth,
        margin : margin + edge,
        margin : margin + edge,
    ]
    local = local.reshape(8, count, edge_depth, edge * edge)
    element_conduct = conduct.reshape(3, count, depth, rows, width)[
        :,
        :,
        margin_depth : margin_depth + edge_depth,
        margin : margin + edge,
        margin : margin + edge,
    ]
    element_conduct = element_conduct.reshape(3, count, edge_depth, edge * edge)
    inner_rows, inner_cols, inner_depth = face_weights(element_conduct, edge, spacing)
    jump = local[..., :-edge] - local[..., edge:]
    stiffness = jnp.einsum(
        "aezn,bezn->eab", jump * inner_rows, jump, precision=lax.Precision.HIGHEST
    )
    jump = local[..., :-1] - local[..., 1:]
    stiffness = stiffness + jnp.einsum(
        "aezn,bezn->eab", jump * inner_cols, jump, precision=lax.Precision.HIGHEST
    )
    jump = local[:, :, :-1] - local[:, :, 1:]
    stiffness = stiffness + jnp.einsum(
        "aezn,bezn->eab", jump * inner_depth, jump, precision=lax.Precision.HIGHEST
    )
    return (local, stiffness)


def coarsen(block):
    comps, rows, width, depth = block.shape
    grouped = block.reshape(comps, rows // 2, 2, width // 2, 2, depth // 2, 2)
    return 0.125 * jnp.sum(grouped, axis=(2, 4, 6))


def corner_stack(corner_first, corner_rows, corner_cols, corner_both, count):
    table = [[corner_first, corner_cols], [corner_rows, corner_both]]
    values = []
    for basis in range(8):
        lift = basis % 2
        values.append(table[basis // 4][basis // 2 % 2][..., lift : lift + count])
    return jnp.stack(values, axis=-1)


def spread(values):
    parts = [[None, None], [None, None]]
    for basis in range(8):
        lift = basis % 2
        widths = [(0, 0)] * (values.ndim - 2) + [(lift, 1 - lift)]
        padded = jnp.pad(values[..., basis], widths)
        first = basis // 4
        second = basis // 2 % 2
        if parts[first][second] is None:
            parts[first][second] = padded
        else:
            parts[first][second] = parts[first][second] + padded
    return parts


def pressure_tile(local, weights, edge):
    combined = jnp.sum(jnp.transpose(weights)[:, :, None, None] * local, axis=0)
    count = combined.shape[0]
    depth = combined.shape[1]
    return jnp.transpose(combined.reshape(count, depth, edge, edge), (2, 3, 0, 1)).reshape(
        edge, edge, count * depth
    )


def neighbours(nodes):
    next_rows = shifted(nodes, "gx", -1)
    fetched = shifted(jnp.stack([nodes[:, 0], next_rows[:, 0]]), "gy", -1)
    next_cols = jnp.concatenate([nodes[:, 1:], fetched[0][:, None]], axis=1)
    next_both = jnp.concatenate([next_rows[:, 1:], fetched[1][:, None]], axis=1)
    return (next_rows, next_cols, next_both)


def local_operator(stiffness, nodes, count):
    next_rows, next_cols, next_both = neighbours(nodes)
    element = corner_stack(nodes, next_rows, next_cols, next_both, count)
    local = jnp.einsum("lckab,lckb->lcka", stiffness, element, precision=lax.Precision.HIGHEST)
    parts = spread(local)
    col_part = parts[0][1]
    both_part = parts[1][1]
    returned = shifted(jnp.stack([col_part[:, -1], both_part[:, -1]]), "gy", 1)
    moved_cols = jnp.concatenate([returned[0][:, None], col_part[:, :-1]], axis=1)
    moved_both = jnp.concatenate([returned[1][:, None], both_part[:, :-1]], axis=1)
    across = shifted(parts[1][0] + moved_both, "gx", 1)
    return parts[0][0] + moved_cols + across


def squares(residual):
    return lax.psum(jnp.sum(residual * residual, axis=(1, 2), keepdims=True), ("gx", "gy"))


def spread_solve(stiffness, columns, count):
    level = jnp.arange(count + 1, dtype=jnp.int32)
    inside = ((level > 0) & (level < count)).astype(jnp.float32)
    boundary = jnp.broadcast_to((level == 0).astype(jnp.float32), (2, columns, count + 1))
    source = -inside * local_operator(stiffness, boundary, count)
    update = jnp.zeros_like(source)
    residual = source
    direction = source
    norm_now = squares(residual)
    for step in range(COARSE_ITERS):
        image = inside * local_operator(stiffness, direction, count)
        alpha = norm_now / lax.psum(
            jnp.sum(direction * image, axis=(1, 2), keepdims=True), ("gx", "gy")
        )
        update = update + alpha * direction
        residual = residual - alpha * image
        norm_next = squares(residual)
        direction = residual + norm_next / norm_now * direction
        norm_now = norm_next
    return boundary + update


def shards(permeability):
    depth_total = ELZ * EZ
    shaped = permeability.reshape(
        3, permeability.shape[1], permeability.shape[2] // depth_total, depth_total
    )
    rimmed = padded_2(shaped, (("gx", 1), ("gy", 2)), MX)
    half_edge = EL // 2
    columns = shaped.shape[2] // EL

    def column_work(offset):
        block = lax.dynamic_slice_in_dim(rimmed, offset, EL + 2 * MX, 2)
        fine_block = jnp.pad(block, ((0, 0), (0, 0), (0, 0), (MZ, MZ)), mode="edge")
        twin_block = coarsen(fine_block)
        fine_local, fine_stiff = solve_column(fine_block, EL, ELZ, MX, MZ, 1.0)
        twin_local, twin_stiff = solve_column(
            twin_block, half_edge, ELZ // 2, MX // 2, MZ // 2, 2.0
        )
        return (fine_local, fine_stiff, twin_local, twin_stiff)

    offsets = jnp.arange(columns, dtype=jnp.int32) * EL
    fine_local, fine_stiff, twin_local, twin_stiff = lax.map(column_work, offsets)
    stiffness = jnp.stack([fine_stiff, twin_stiff])
    count = stiffness.shape[2]
    corner_first = spread_solve(stiffness, columns, count)
    corner_rows, corner_cols, corner_both = neighbours(corner_first)
    weights = corner_stack(corner_first, corner_rows, corner_cols, corner_both, count)
    fine_tiles = [
        pressure_tile(fine_local[column], weights[0, column], EL) for column in range(columns)
    ]
    twin_tiles = [
        pressure_tile(twin_local[column], weights[1, column], half_edge)
        for column in range(columns)
    ]
    fine_pressure = jnp.concatenate(fine_tiles, axis=1)
    twin_pressure = jnp.concatenate(twin_tiles, axis=1)
    return (fine_pressure.reshape(EL, -1), twin_pressure.reshape(half_edge, -1))


def solution(mesh):
    placed = (P(None, "gx", "gy"),)
    return jax.shard_map(
        shards,
        mesh=mesh,
        in_specs=placed,
        out_specs=(P("gx", "gy"), P("gx", "gy")),
        check_vma=False,
    )
```

profile of v0, /device:TPU:1, one launch (start us, length us, event | category | flops | bytes accessed | tf_op | source)
XLA Modules:
  0.0 635.2 jit_solution(149568154038995864)
XLA Ops:
  0.6 2.1 reshape.1460
  3.7 2.5 collective-permute-start
  6.1 3.9 collective-permute-start.1
  13.8 4.4 collective-permute-done.4
  21.2 2.5 collective-permute-done.5
  25.7 1.9 copy-done.12
  27.6 2.6 collective-permute-start.3
  32.8 2.7 copy.335
  35.6 2.1 copy.336
  37.6 2.0 copy.334
  39.7 4.5 pad_maximum_fusion.3
  44.2 299.3 %while.21 = (s32[]{:T(128)}, f32[2,8,2,16,1024]{4,1,3,2,0:T(8,128)}, f32[2,2,8,8]{3,2,1,0:T(8,128)}, f32[2,8,2,8,256]{4,1,3,2,0:T(8,128)}, f32[2,2,8,8]{3,2,1,0:...) while((s32[]{:T(128)}, ...), condition=%wide.region_14.15_spmd, body=%wide.region_0.14_spmd.sunk | while | flops 130577320 | bytes 255059728 | solution.py:275
  45.1 1.7 stack.282
  50.3 2.1 constant_dynamic-slice_fusion.2
  62.3 2.2 reshape.1501
  66.1 1.6 broadcast_multiply_fusion.34
  69.1 2.2 reshape.1502
  88.3 2.0 add_add_fusion.5
  90.3 5.9 reshape.1503
  96.2 5.7 slice.2293
  102.0 3.7 broadcast_in_dim.249
  106.8 3.9 reshape.1504
  110.7 2.9 fusion.260
  113.6 1.9 squeeze.279
  116.6 2.3 fusion.261
  118.9 1.9 squeeze.280
  121.9 2.5 fusion.262
  126.4 3.0 fusion.264
  131.4 26.2 %reshape.1505 = f32[3,20,2,20,2,18,2]{4,3,2,1,6,5,0:T(8,128)} reshape(f32[3,40,40,36]{2,1,3,0:T(8,128)} %pad_maximum_fusion.26) | data formatting | bytes 1382400 | tf_op jit(solution)/shard_map/while/body/eval_jaxpr/reshape | solution.py:170
  157.7 19.5 %reduce_sum.329 = f32[3,20,20,18]{2,1,3,0:T(8,128)S(1)} reduce(f32[3,20,2,20,2,18,2]{4,3,2,1,6,5,0:T(8,128)} %reshape.1505, f32[]{:T(128)} %constant.340.clone.31..sunk), dimensions={2,4,6}, to_apply=%region_7.7 | reduce | flops 151200 | bytes 777604 | tf_op jit(solution)/shard_map/while/body/eval_jaxpr/reduce_sum | solution.py:171
  182.1 1.9 reshape.1506
  184.0 1.8 slice.2294
  190.5 1.7 stack.282
  195.8 2.1 constant_dynamic-slice_fusion.2
  207.8 2.2 reshape.1501
  214.6 2.2 reshape.1502
  233.5 2.0 add_add_fusion.5
  235.5 5.9 reshape.1503
  241.5 5.7 slice.2293
  247.2 3.7 broadcast_in_dim.249
  252.0 4.0 reshape.1504
  256.0 2.9 fusion.260
  258.9 1.9 squeeze.279
  261.8 2.3 fusion.261
  264.1 1.9 squeeze.280
  267.2 2.5 fusion.262
  271.7 3.0 fusion.264
  276.7 26.2 %reshape.1505 = f32[3,20,2,20,2,18,2]{4,3,2,1,6,5,0:T(8,128)} reshape(f32[3,40,40,36]{2,1,3,0:T(8,128)} %pad_maximum_fusion.26) | data formatting | bytes 1382400 | tf_op jit(solution)/shard_map/while/body/eval_jaxpr/reshape | solution.py:170
  302.9 19.7 %reduce_sum.329 = f32[3,20,20,18]{2,1,3,0:T(8,128)S(1)} reduce(f32[3,20,2,20,2,18,2]{4,3,2,1,6,5,0:T(8,128)} %reshape.1505, f32[]{:T(128)} %constant.340.clone.31..sunk), dimensions={2,4,6}, to_apply=%region_7.7 | reduce | flops 151200 | bytes 777604 | tf_op jit(solution)/shard_map/while/body/eval_jaxpr/reduce_sum | solution.py:171
  327.6 1.9 reshape.1506
  329.5 1.8 slice.2294
  344.9 7.2 %collective-permute-done.6 = f32[2,2,3]{2,1,0:T(2,128)S(1)} collective-permute-done((f32[2,2,3]{2,1,0:T(2,128)S(1)}, f32[2,2,3]{2,1,0:T(2,128)S(1)}, u32[]{:S(2)}, u32[]{:S(2)}) %collective-permute-start.6) | collective-permute-done | bytes 80 | tf_op jit(solution)/shard_map/ppermute | solution.py:17
  352.2 4.6 collective-permute-done.7
  360.1 7.4 %collective-permute-start.9 = (f32[2,2,3]{2,1,0:T(2,128)S(1)}, f32[2,2,3]{2,1,0:T(2,128)S(1)}, u32[]{:S(2)}, u32[]{:S(2)}) collective-permute-start(f32[2,2,3]{2,1,0:T(2,128)S(1)} %pad_maximum_fusion.20), channel_id=1, source_target_pairs={{0,31},{1,0},{2,1},{3,2},{4,3},{5,4},{6,5},{7,6},{8,7},{9,8},{10,9... | collective-permute-start | bytes 152 | tf_op jit(solution)/shard_map/ppermute | solution.py:17
  371.6 4.2 collective-permute-done.11
  376.6 77.9 %all-reduce.72 = (f32[2,1,1]{0,2,1:T(1,128)S(1)}, f32[2,1,1]{0,2,1:T(1,128)S(1)}) all-reduce(f32[2,1,1]{0,2,1:T(1,128)S(1)} %bitcast.449, f32[2,1,1]{0,2,1:T(1,128)S(1)} %bitcast.448), channel_id=1, replica_groups=mesh['gx'=8,'gy'=32] {'gx','gy'}, use_global_device_ids=true, to_apply=%region_16.17 | all-reduce | flops 4 | bytes 32 | tf_op jit(solution)/shard_map/psum | solution.py:230
  454.7 73.6 %psum.30 = f32[2,1,1]{0,2,1:T(1,128)S(1)} all-reduce(f32[2,1,1]{0,2,1:T(1,128)S(1)} %bitcast.451), channel_id=1, replica_groups=mesh['gx'=8,'gy'=32] {'gx','gy'}, use_global_device_ids=true, to_apply=%region_20.21 | all-reduce | flops 2 | bytes 16 | tf_op jit(solution)/shard_map/psum | solution.py:230
  528.5 1.7 collective-permute-start.12
  533.1 2.0 collective-permute-done.13
  538.3 1.7 collective-permute-start.15
  540.0 2.5 collective-permute-done.15
  543.3 77.1 %psum.31 = f32[2,1,1]{0,2,1:T(1,128)S(1)} all-reduce(f32[2,1,1]{0,2,1:T(1,128)S(1)} %bitcast.450), channel_id=1, replica_groups=mesh['gx'=8,'gy'=32] {'gx','gy'}, use_global_device_ids=true, to_apply=%region_22.23 | all-reduce | flops 2 | bytes 16 | tf_op jit(solution)/shard_map/psum | solution.py:244
  623.9 1.8 collective-permute-start.17
  628.3 2.3 fusion.116
  (519 shorter events, 135.0 us)
Async XLA Ops:
  3.7 20.6 %collective-permute-start = (f32[3,4,64,32]{3,2,1,0:T(8,128)}, f32[3,4,64,32]{3,2,1,0:T(8,128)}, u32[]{:S(2)}, u32[]{:S(2)}) collective-permute-start(f32[3,4,64,32]{3,2,1,0:T(8,128)} %get-tuple-element.370), channel_id=1, source_target_pairs={{0,32},{32,64},{64,96},{96,128},{128,160},{160,192},{192,224},{224... | collective-permute-start | bytes 294920 | tf_op jit(solution)/shard_map/ppermute | solution.py:27
  6.1 19.5 %collective-permute-start.1 = (f32[3,4,64,32]{3,2,1,0:T(8,128)}, f32[3,4,64,32]{3,2,1,0:T(8,128)S(1)}, u32[]{:S(2)}, u32[]{:S(2)}) collective-permute-start(f32[3,4,64,32]{3,2,1,0:T(8,128)} %get-tuple-element.369), channel_id=1, source_target_pairs={{32,0},{64,32},{96,64},{128,96},{160,128},{192,160},{224,192},{0,2... | collective-permute-start | bytes 294920 | tf_op jit(solution)/shard_map/ppermute | solution.py:29
  10.1 20.1 %copy-start.18 = (f32[3]{0:T(128)}, f32[3]{0:T(128)S(1)}, u32[]{:S(2)}) copy-start(f32[3]{0:T(128)S(1)} %compare_convert_fusion) | copy-start | bytes 40
  10.1 8.1 %collective-permute-start.4 = (f32[2,2,3]{2,0,1:T(2,128)S(1)}, f32[2,2,3]{2,0,1:T(2,128)S(1)}, u32[]{:S(2)}, u32[]{:S(2)}) collective-permute-start(f32[2,2,3]{2,0,1:T(2,128)S(1)} %broadcast_in_dim.227), channel_id=1, source_target_pairs={{0,224},{32,0},{64,32},{96,64},{128,96},{160,128},{192,160},{224,1... | collective-permute-start | bytes 152 | tf_op jit(solution)/shard_map/ppermute | solution.py:17
  19.3 4.3 collective-permute-start.5
  25.4 4.9 copy-start.19
  25.6 1.9 copy-start.12
  27.6 7.9 %collective-permute-start.3 = (f32[3,40,4,32]{3,2,1,0:T(4,128)S(1)}, f32[3,40,4,32]{3,2,1,0:T(4,128)S(1)}, u32[]{:S(2)}, u32[]{:S(2)}) collective-permute-start(f32[3,40,4,32]{3,2,1,0:T(4,128)S(1)} %get-tuple-element.368), channel_id=1, source_target_pairs={{1,0},{2,1},{3,2},{4,3},{5,4},{6,5},{7,6},{8,7},{9,8},{10,9},{11,1... | collective-permute-start | bytes 184328 | tf_op jit(solution)/shard_map/ppermute | solution.py:29
  30.2 7.4 %collective-permute-start.2 = (f32[3,40,4,32]{3,2,1,0:T(4,128)S(1)}, f32[3,40,4,32]{3,2,1,0:T(4,128)S(1)}, u32[]{:S(2)}, u32[]{:S(2)}) collective-permute-start(f32[3,40,4,32]{3,2,1,0:T(4,128)S(1)} %get-tuple-element.367), channel_id=1, source_target_pairs={{0,1},{1,2},{2,3},{3,4},{4,5},{5,6},{6,7},{7,8},{8,9},{9,10},{10,1... | collective-permute-start | bytes 184328 | tf_op jit(solution)/shard_map/ppermute | solution.py:27
  39.7 4.5 copy-start.20
  53.6 0.6 copy-start.8
  53.7 0.7 copy-start.10
  54.5 2.3 copy-start
  58.3 1.2 copy-start.7
  64.5 1.6 copy-start.5
  66.1 3.0 copy-start.3
  71.3 1.6 copy-start.6
  72.8 1.6 copy-start.1
  72.8 2.2 copy-start.2
  76.3 1.0 copy-start.4
  125.3 4.6 copy-start.9
  125.3 4.6 copy-start.11
  184.0 2.2 copy-start.13
  185.8 2.6 copy-start.16
  186.3 3.2 copy-start.21
  186.3 2.6 copy-start.14
  188.9 0.6 copy-start.17
  199.1 0.6 copy-start.8
  199.1 0.7 copy-start.10
  199.9 2.3 copy-start
  203.7 1.2 copy-start.7
  210.0 1.6 copy-start.5
  211.6 3.0 copy-start.3
  216.7 1.6 copy-start.6
  218.3 1.6 copy-start.1
  218.3 2.2 copy-start.2
  221.8 1.0 copy-start.4
  270.5 4.6 copy-start.9
  270.5 4.6 copy-start.11
  329.5 2.2 copy-start.13
  331.3 2.6 copy-start.16
  331.8 3.2 copy-start.21
  331.8 2.6 copy-start.14
  334.3 0.6 copy-start.17
  344.8 7.3 %collective-permute-start.6 = (f32[2,2,3]{2,1,0:T(2,128)S(1)}, f32[2,2,3]{2,1,0:T(2,128)S(1)}, u32[]{:S(2)}, u32[]{:S(2)}) collective-permute-start(f32[2,2,3]{2,1,0:T(2,128)S(1)} %pad_maximum_fusion.19), channel_id=1, source_target_pairs={{0,1},{1,2},{2,3},{3,4},{4,5},{5,6},{6,7},{7,8},{8,9},{9,10},{10,1... | collective-permute-start | bytes 152 | tf_op jit(solution)/shard_map/ppermute | solution.py:17
  352.2 4.6 collective-permute-start.7
  357.6 2.4 collective-permute-start.8
  360.1 8.2 %collective-permute-start.9 = (f32[2,2,3]{2,1,0:T(2,128)S(1)}, f32[2,2,3]{2,1,0:T(2,128)S(1)}, u32[]{:S(2)}, u32[]{:S(2)}) collective-permute-start(f32[2,2,3]{2,1,0:T(2,128)S(1)} %pad_maximum_fusion.20), channel_id=1, source_target_pairs={{0,31},{1,0},{2,1},{3,2},{4,3},{5,4},{6,5},{7,6},{8,7},{9,8},{10,9... | collective-permute-start | bytes 152 | tf_op jit(solution)/shard_map/ppermute | solution.py:17
  370.2 1.2 collective-permute-start.10
  371.5 4.2 collective-permute-start.11
  528.5 2.7 collective-permute-start.12
  531.2 3.9 collective-permute-start.13
  537.0 1.2 collective-permute-start.14
  538.3 4.2 collective-permute-start.15
  621.2 2.7 collective-permute-start.16
  623.9 3.7 collective-permute-start.17
  631.5 1.8 copy-start.15
where the time goes:
time: 646 us; the launch traced here: 635 us
  blocking collectives  229 us (35%)
  local copies, waits for them, and re-layouts  188 us (29%)
  other arithmetic  118 us (18%)
  waiting for transfers between devices  34.7 us (5%)
  starting transfers between devices  28.8 us (4%)
  matrix products  20.8 us (3%)
  loops' own time  14.6 us (2%)
    psum x2, blocking collectives, squares(): lax.psum(jnp.sum(residual * residual, axis=(1, 2), keepdims=True), ('gx',...  152 us
    psum x1, blocking collectives, spread_solve(): lax.psum(jnp.sum(direction * image, axis=(1, 2), keepdims=True), ('gx', '...  77.1 us
    reshape x2, local copies, waits for them, and re-layouts, coarsen(): grouped = block.reshape(comps, rows // 2, 2, width // 2, 2, depth // 2, 2)  52.5 us
    reduce_sum x2, other arithmetic, coarsen(): return 0.125 * jnp.sum(grouped, axis=(2, 4, 6))  39.3 us
    ppermute x14, waiting for transfers between devices, shifted(): lax.ppermute(shard, axis, [(i, (i + by) % count) for i in range(count)])  34.7 us
    ppermute x14, starting transfers between devices, shifted(): lax.ppermute(shard, axis, [(i, (i + by) % count) for i in range(count)])  19.8 us
    reshape x4, local copies, waits for them, and re-layouts, solve_column(): solution.reshape(8, count, depth, rows, width)  15.7 us
    slice x4, local copies, waits for them, and re-layouts, solve_column(): solution.reshape(8, count, depth, rows, width)  15 us
  transfers between devices with their start and end apart: 18, of which 14 were waited for; matrix products, arithmetic and copies ran while one was open for 2% of the time, Pallas kernels for 0%

commit v1 on v0

--- a/solution.py
+++ b/solution.py
@@ -227,7 +227,7 @@
 
 
 def squares(residual):
-    return lax.psum(jnp.sum(residual * residual, axis=(1, 2), keepdims=True), ("gx", "gy"))
+    return lax.psum(lax.psum(jnp.sum(residual * residual, axis=(1, 2), keepdims=True), "gx"), "gy")
 
 
 def spread_solve(stiffness, columns, count):

time: 646 us -> 729 us (1.13)
  blocking collectives: 229 us -> 313 us
    psum x1 -> x2, blocking collectives: 77.1 us -> 149 us  [spread_solve(): lax.psum(jnp.sum(direction * image, axis=(1, 2), keepdims=True), ('gx', '...]
    psum x2 -> x4, blocking collectives: 152 us -> 164 us  [the longest x2 139 us: squares(): lax.psum(lax.psum(jnp.sum(residual * residual, axis=(1, 2), keepdims=True...]
where the time goes in v1:
time: 729 us; the launch traced here: 718 us
  blocking collectives  313 us (43%)
  local copies, waits for them, and re-layouts  187 us (26%)
  other arithmetic  119 us (16%)
  waiting for transfers between devices  36.6 us (5%)
  starting transfers between devices  26.2 us (4%)
  matrix products  20.8 us (3%)
  loops' own time  14.7 us (2%)
    psum x2, blocking collectives, spread_solve(): lax.psum(jnp.sum(direction * image, axis=(1, 2), keepdims=True), ('gx', '...  149 us
    psum x2, blocking collectives, squares(): lax.psum(lax.psum(jnp.sum(residual * residual, axis=(1, 2), keepdims=True...  139 us
    reshape x2, local copies, waits for them, and re-layouts, coarsen(): grouped = block.reshape(comps, rows // 2, 2, width // 2, 2, depth // 2, 2)  52.3 us
    reduce_sum x2, other arithmetic, coarsen(): return 0.125 * jnp.sum(grouped, axis=(2, 4, 6))  39.3 us
    ppermute x14, waiting for transfers between devices, shifted(): lax.ppermute(shard, axis, [(i, (i + by) % count) for i in range(count)])  36.6 us
    psum x2, blocking collectives, squares(): lax.psum(jnp.sum(residual * residual, axis=(1, 2), keepdims=True), 'gx')  24.9 us
    ppermute x14, starting transfers between devices, shifted(): lax.ppermute(shard, axis, [(i, (i + by) % count) for i in range(count)])  17.2 us
    reshape x4, local copies, waits for them, and re-layouts, solve_column(): solution.reshape(8, count, depth, rows, width)  15.6 us
  transfers between devices with their start and end apart: 18, of which 14 were waited for; matrix products, arithmetic and copies ran while one was open for 2% of the time, Pallas kernels for 0%

profile of v1, /device:TPU:1, one launch (start us, length us, event | category | flops | bytes accessed | tf_op | source)
XLA Modules:
  0.0 718.5 jit_solution(4387477098462574562)
XLA Ops:
  0.6 2.1 reshape.1460
  3.7 2.5 collective-permute-start
  6.1 3.9 collective-permute-start.1
  13.8 4.4 collective-permute-done.4
  21.2 2.5 collective-permute-done.5
  25.6 1.9 copy-done.12
  27.6 2.6 collective-permute-start.3
  32.9 2.7 copy.335
  35.6 2.1 copy.336
  37.7 2.1 copy.334
  39.8 4.5 pad_maximum_fusion.3
  44.3 299.0 %while.21 = (s32[]{:T(128)}, f32[2,8,2,16,1024]{4,1,3,2,0:T(8,128)}, f32[2,2,8,8]{3,2,1,0:T(8,128)}, f32[2,8,2,8,256]{4,1,3,2,0:T(8,128)}, f32[2,2,8,8]{3,2,1,0:...) while((s32[]{:T(128)}, ...), condition=%wide.region_14.15_spmd, body=%wide.region_0.14_spmd.sunk | while | flops 130577320 | bytes 255059728 | solution.py:275
  50.4 2.1 constant_dynamic-slice_fusion.2
  62.4 2.1 reshape.1501
  69.1 2.1 reshape.1502
  88.3 2.0 add_add_fusion.5
  90.3 5.9 reshape.1503
  96.2 5.7 slice.2293
  101.9 3.7 broadcast_in_dim.249
  106.7 3.9 reshape.1504
  110.6 2.9 fusion.260
  113.6 1.9 squeeze.279
  116.5 2.3 fusion.261
  118.8 1.9 squeeze.280
  121.8 2.5 fusion.262
  126.3 3.0 fusion.264
  131.4 26.2 %reshape.1505 = f32[3,20,2,20,2,18,2]{4,3,2,1,6,5,0:T(8,128)} reshape(f32[3,40,40,36]{2,1,3,0:T(8,128)} %pad_maximum_fusion.26) | data formatting | bytes 1382400 | tf_op jit(solution)/shard_map/while/body/eval_jaxpr/reshape | solution.py:170
  157.6 19.5 %reduce_sum.329 = f32[3,20,20,18]{2,1,3,0:T(8,128)S(1)} reduce(f32[3,20,2,20,2,18,2]{4,3,2,1,6,5,0:T(8,128)} %reshape.1505, f32[]{:T(128)} %constant.340.clone.31..sunk), dimensions={2,4,6}, to_apply=%region_7.7 | reduce | flops 151200 | bytes 777604 | tf_op jit(solution)/shard_map/while/body/eval_jaxpr/reduce_sum | solution.py:171
  182.0 1.9 reshape.1506
  184.0 1.8 slice.2294
  195.7 2.1 constant_dynamic-slice_fusion.2
  207.6 2.1 reshape.1501
  214.4 2.1 reshape.1502
  233.3 2.0 add_add_fusion.5
  235.4 5.9 reshape.1503
  241.3 5.7 slice.2293
  247.0 3.7 broadcast_in_dim.249
  251.8 4.0 reshape.1504
  255.8 2.9 fusion.260
  258.7 1.9 squeeze.279
  261.6 2.3 fusion.261
  263.9 1.9 squeeze.280
  267.0 2.5 fusion.262
  271.5 3.0 fusion.264
  276.5 26.2 %reshape.1505 = f32[3,20,2,20,2,18,2]{4,3,2,1,6,5,0:T(8,128)} reshape(f32[3,40,40,36]{2,1,3,0:T(8,128)} %pad_maximum_fusion.26) | data formatting | bytes 1382400 | tf_op jit(solution)/shard_map/while/body/eval_jaxpr/reshape | solution.py:170
  302.7 19.7 %reduce_sum.329 = f32[3,20,20,18]{2,1,3,0:T(8,128)S(1)} reduce(f32[3,20,2,20,2,18,2]{4,3,2,1,6,5,0:T(8,128)} %reshape.1505, f32[]{:T(128)} %constant.340.clone.31..sunk), dimensions={2,4,6}, to_apply=%region_7.7 | reduce | flops 151200 | bytes 777604 | tf_op jit(solution)/shard_map/while/body/eval_jaxpr/reduce_sum | solution.py:171
  327.4 1.9 reshape.1506
  329.3 1.8 slice.2294
  344.6 7.2 collective-permute-done.6
  351.9 4.6 collective-permute-done.7
  359.8 7.4 %collective-permute-start.9 = (f32[2,2,3]{2,1,0:T(2,128)S(1)}, f32[2,2,3]{2,1,0:T(2,128)S(1)}, u32[]{:S(2)}, u32[]{:S(2)}) collective-permute-start(f32[2,2,3]{2,1,0:T(2,128)S(1)} %pad_maximum_fusion.20), channel_id=1, source_target_pairs={{0,31},{1,0},{2,1},{3,2},{4,3},{5,4},{6,5},{7,6},{8,7},{9,8},{10,9... | collective-permute-start | bytes 152 | tf_op jit(solution)/shard_map/ppermute | solution.py:17
  371.2 4.2 collective-permute-done.11
  376.3 12.0 %psum.42 = f32[2,1,1]{0,2,1:T(1,128)S(1)} all-reduce(f32[2,1,1]{0,2,1:T(1,128)S(1)} %bitcast.449), channel_id=1, replica_groups=mesh['gx'=8,'gy'=32] {'gx'}, use_global_device_ids=true, to_apply=%region_16.17 | all-reduce | flops 2 | bytes 16 | tf_op jit(solution)/shard_map/psum | solution.py:230
  388.3 72.4 %psum.43 = f32[2,1,1]{0,2,1:T(1,128)S(1)} all-reduce(f32[2,1,1]{0,2,1:T(1,128)S(1)} %psum.42), channel_id=1, replica_groups=mesh['gx'=8,'gy'=32] {'gy'}, use_global_device_ids=true, to_apply=%region_17.18 | all-reduce | flops 2 | bytes 16 | tf_op jit(solution)/shard_map/psum | solution.py:230
  460.7 72.6 %psum.44 = f32[2,1,1]{0,2,1:T(1,128)S(1)} all-reduce(f32[2,1,1]{0,2,1:T(1,128)S(1)} %bitcast.448), channel_id=1, replica_groups=mesh['gx'=8,'gy'=32] {'gx','gy'}, use_global_device_ids=true, to_apply=%region_19.20 | all-reduce | flops 2 | bytes 16 | tf_op jit(solution)/shard_map/psum | solution.py:244
  533.5 12.9 %psum.45 = f32[2,1,1]{0,2,1:T(1,128)S(1)} all-reduce(f32[2,1,1]{0,2,1:T(1,128)S(1)} %bitcast.451), channel_id=1, replica_groups=mesh['gx'=8,'gy'=32] {'gx'}, use_global_device_ids=true, to_apply=%region_21.22 | all-reduce | flops 2 | bytes 16 | tf_op jit(solution)/shard_map/psum | solution.py:230
  546.4 66.4 %psum.46 = f32[2,1,1]{0,2,1:T(1,128)S(1)} all-reduce(f32[2,1,1]{0,2,1:T(1,128)S(1)} %psum.45), channel_id=1, replica_groups=mesh['gx'=8,'gy'=32] {'gy'}, use_global_device_ids=true, to_apply=%region_22.23 | all-reduce | flops 2 | bytes 16 | tf_op jit(solution)/shard_map/psum | solution.py:230
  613.3 2.2 collective-permute-done.12
  615.5 1.8 collective-permute-start.13
  621.8 3.9 collective-permute-done.15
  626.5 76.5 %psum.47 = f32[2,1,1]{0,2,1:T(1,128)S(1)} all-reduce(f32[2,1,1]{0,2,1:T(1,128)S(1)} %bitcast.450), channel_id=1, replica_groups=mesh['gx'=8,'gy'=32] {'gx','gy'}, use_global_device_ids=true, to_apply=%region_24.25 | all-reduce | flops 2 | bytes 16 | tf_op jit(solution)/shard_map/psum | solution.py:244
  703.9 1.8 collective-permute-start.16
  708.7 2.1 collective-permute-done.17
  711.6 2.3 fusion.116
  (522 shorter events, 137.1 us)
Async XLA Ops:
  3.7 20.6 %collective-permute-start = (f32[3,4,64,32]{3,2,1,0:T(8,128)}, f32[3,4,64,32]{3,2,1,0:T(8,128)}, u32[]{:S(2)}, u32[]{:S(2)}) collective-permute-start(f32[3,4,64,32]{3,2,1,0:T(8,128)} %get-tuple-element.368), channel_id=1, source_target_pairs={{0,32},{32,64},{64,96},{96,128},{128,160},{160,192},{192,224},{224... | collective-permute-start | bytes 294920 | tf_op jit(solution)/shard_map/ppermute | solution.py:27
  6.1 19.4 %collective-permute-start.1 = (f32[3,4,64,32]{3,2,1,0:T(8,128)}, f32[3,4,64,32]{3,2,1,0:T(8,128)S(1)}, u32[]{:S(2)}, u32[]{:S(2)}) collective-permute-start(f32[3,4,64,32]{3,2,1,0:T(8,128)} %get-tuple-element.367), channel_id=1, source_target_pairs={{32,0},{64,32},{96,64},{128,96},{160,128},{192,160},{224,192},{0,2... | collective-permute-start | bytes 294920 | tf_op jit(solution)/shard_map/ppermute | solution.py:29
  10.1 20.1 %copy-start.18 = (f32[3]{0:T(128)}, f32[3]{0:T(128)S(1)}, u32[]{:S(2)}) copy-start(f32[3]{0:T(128)S(1)} %compare_convert_fusion) | copy-start | bytes 40
  10.1 8.1 %collective-permute-start.4 = (f32[2,2,3]{2,0,1:T(2,128)S(1)}, f32[2,2,3]{2,0,1:T(2,128)S(1)}, u32[]{:S(2)}, u32[]{:S(2)}) collective-permute-start(f32[2,2,3]{2,0,1:T(2,128)S(1)} %broadcast_in_dim.227), channel_id=1, source_target_pairs={{0,224},{32,0},{64,32},{96,64},{128,96},{160,128},{192,160},{224,1... | collective-permute-start | bytes 152 | tf_op jit(solution)/shard_map/ppermute | solution.py:17
  19.3 4.3 collective-permute-start.5
  25.3 4.9 copy-start.19
  25.6 1.9 copy-start.12
  27.6 8.0 %collective-permute-start.3 = (f32[3,40,4,32]{3,2,1,0:T(4,128)S(1)}, f32[3,40,4,32]{3,2,1,0:T(4,128)S(1)}, u32[]{:S(2)}, u32[]{:S(2)}) collective-permute-start(f32[3,40,4,32]{3,2,1,0:T(4,128)S(1)} %get-tuple-element.366), channel_id=1, source_target_pairs={{1,0},{2,1},{3,2},{4,3},{5,4},{6,5},{7,6},{8,7},{9,8},{10,9},{11,1... | collective-permute-start | bytes 184328 | tf_op jit(solution)/shard_map/ppermute | solution.py:29
  30.2 7.5 %collective-permute-start.2 = (f32[3,40,4,32]{3,2,1,0:T(4,128)S(1)}, f32[3,40,4,32]{3,2,1,0:T(4,128)S(1)}, u32[]{:S(2)}, u32[]{:S(2)}) collective-permute-start(f32[3,40,4,32]{3,2,1,0:T(4,128)S(1)} %get-tuple-element.365), channel_id=1, source_target_pairs={{0,1},{1,2},{2,3},{3,4},{4,5},{5,6},{6,7},{7,8},{8,9},{9,10},{10,1... | collective-permute-start | bytes 184328 | tf_op jit(solution)/shard_map/ppermute | solution.py:27
  39.8 4.5 copy-start.20
  53.7 0.6 copy-start.8
  53.8 0.7 copy-start.10
  54.6 2.3 copy-start
  58.3 1.2 copy-start.7
  64.5 1.6 copy-start.5
  66.1 3.0 copy-start.3
  71.3 1.6 copy-start.6
  72.8 1.6 copy-start.1
  72.8 2.2 copy-start.2
  76.3 1.0 copy-start.4
  125.2 4.6 copy-start.9
  125.2 4.6 copy-start.11
  183.9 2.2 copy-start.13
  185.7 2.6 copy-start.16
  186.2 3.2 copy-start.21
  186.2 2.6 copy-start.14
  188.8 0.6 copy-start.17
  199.0 0.6 copy-start.8
  199.0 0.7 copy-start.10
  199.9 2.3 copy-start
  203.6 1.2 copy-start.7
  209.8 1.6 copy-start.5
  211.4 3.0 copy-start.3
  216.5 1.6 copy-start.6
  218.1 1.6 copy-start.1
  218.1 2.2 copy-start.2
  221.6 1.0 copy-start.4
  270.3 4.6 copy-start.9
  270.3 4.6 copy-start.11
  329.3 2.2 copy-start.13
  331.1 2.6 copy-start.16
  331.5 3.2 copy-start.21
  331.5 2.6 copy-start.14
  334.1 0.6 copy-start.17
  344.6 7.3 %collective-permute-start.6 = (f32[2,2,3]{2,1,0:T(2,128)S(1)}, f32[2,2,3]{2,1,0:T(2,128)S(1)}, u32[]{:S(2)}, u32[]{:S(2)}) collective-permute-start(f32[2,2,3]{2,1,0:T(2,128)S(1)} %pad_maximum_fusion.19), channel_id=1, source_target_pairs={{0,1},{1,2},{2,3},{3,4},{4,5},{5,6},{6,7},{7,8},{8,9},{9,10},{10,1... | collective-permute-start | bytes 152 | tf_op jit(solution)/shard_map/ppermute | solution.py:17
  351.9 4.6 collective-permute-start.7
  357.3 2.4 collective-permute-start.8
  359.8 8.2 %collective-permute-start.9 = (f32[2,2,3]{2,1,0:T(2,128)S(1)}, f32[2,2,3]{2,1,0:T(2,128)S(1)}, u32[]{:S(2)}, u32[]{:S(2)}) collective-permute-start(f32[2,2,3]{2,1,0:T(2,128)S(1)} %pad_maximum_fusion.20), channel_id=1, source_target_pairs={{0,31},{1,0},{2,1},{3,2},{4,3},{5,4},{6,5},{7,6},{8,7},{9,8},{10,9... | collective-permute-start | bytes 152 | tf_op jit(solution)/shard_map/ppermute | solution.py:17
  369.9 1.2 collective-permute-start.10
  371.2 4.2 collective-permute-start.11
  613.0 2.5 collective-permute-start.12
  615.5 3.0 collective-permute-start.13
  620.4 1.2 collective-permute-start.14
  621.7 4.0 collective-permute-start.15
  703.9 2.8 collective-permute-start.16
  706.7 4.2 collective-permute-start.17
  714.8 1.8 copy-start.15
